TPU v7x, 32 devices: a whole 2x2x4 slice. The times are simulated.
32 devices in a mesh: groups: 2 (over y), ctx: 4 (over x, core), mp: 4 (over z).
Axes of the slice: x: 2, y: 2, z: 4, core: 2. Of those that a mesh axis runs over, the one named last changes fastest.
Arguments:
- tokens: bfloat16 [3072, 8192], P(('groups', 'ctx')), parts along dimension 0, may hold values from -6 to 6
- norm_gain: bfloat16 [8192], replicated, may hold values from 0.099609375 to 1.8984375
- w_query: bfloat16 [8192, 4096], P('ctx', 'mp'), may hold values from -0.44194174 to 0.44194174
- w_key: bfloat16 [8192, 1024], P('ctx', 'mp'), may hold values from -0.044194174 to 0.044194174
- value_weight: bfloat16 [8192, 1024], P('ctx', 'mp'), may hold values from -0.0625 to 0.0625
- slab_order: int32 [8], P('groups'), parts along dimension 0, may hold values from 0 to 3, each once
- segment_ids: int32 [3072], P('groups'), parts along dimension 0, may hold values from 0 to 3, as said below
Outputs:
- attended: bfloat16 [3072, 4096], P(('groups', 'ctx'), 'mp'), parts along dimension 0
There are 2 independent parts, one for each index of `groups`. A program takes and returns all parts, laid end to end along the dimension named above; an argument that names none is the same for every part. Nothing has to cross between parts.
Inputs may be any that keep to these rules, and one draw needn't show every extreme that they name: `segment_ids`: never falling along positions; each of the 4 segments holds at least one position.
All inputs are finite; a program needn't handle non-finite values.
Results may differ from a plain program's by a relative error of at most 0.012.
Values may be sent and summed in bfloat16 or wider, within the bound.
A program may use at most 128 MiB of HBM per device.

v0:
```python
import math
import jax
import jax.numpy as jnp
from jax import lax
from jax.sharding import PartitionSpec as P

HEAD_SIZE = 128


def apply_rotary(values, positions, heads):
    width = values.shape[1] // heads
    half = width // 2
    freqs = jnp.exp(jnp.arange(half, dtype=jnp.float32) * (-2.0 * math.log(500000.0) / width))
    angles = positions.astype(jnp.float32)[:, None] * freqs[None, :]
    cosine = jnp.cos(angles)[:, None, :]
    sine = jnp.sin(angles)[:, None, :]
    shaped = values.reshape(values.shape[0], heads, width)
    first = shaped[..., :half]
    second = shaped[..., half:]
    turned = jnp.concatenate(
        [first * cosine - second * sine, second * cosine + first * sine], axis=-1
    )
    return turned.reshape(values.shape)


def local(tokens, norm_gain, w_query, w_key, value_weight, slab_order, segment_ids):
    tok_rows = tokens.shape[0]
    device_slab = lax.axis_index("ctx")
    position_all = (
        slab_order[:, None] * tok_rows + jnp.arange(tok_rows, dtype=jnp.int32)[None, :]
    ).reshape(-1)
    segment_all = jnp.take(segment_ids, position_all)
    my_position = lax.dynamic_slice_in_dim(position_all, device_slab * tok_rows, tok_rows)
    my_segment = lax.dynamic_slice_in_dim(segment_all, device_slab * tok_rows, tok_rows)
    floats = tokens.astype(jnp.float32)
    inverse = lax.rsqrt(jnp.mean(floats * floats, axis=-1, keepdims=True) + 1e-05)
    normed = (floats * inverse * norm_gain.astype(jnp.float32)[None, :]).astype(jnp.bfloat16)
    query_cols = w_query.shape[1]
    key_cols = w_key.shape[1]
    query = jnp.dot(
        normed,
        lax.all_gather(w_query, "ctx", axis=0, tiled=True),
        preferred_element_type=jnp.float32,
    )
    key_projected = jnp.dot(
        normed, lax.all_gather(w_key, "ctx", axis=0, tiled=True), preferred_element_type=jnp.float32
    )
    value_proj = jnp.dot(
        normed,
        lax.all_gather(value_weight, "ctx", axis=0, tiled=True),
        preferred_element_type=jnp.float32,
    )
    head_size = HEAD_SIZE
    heads_here = query_cols // head_size
    kv_here = key_cols // head_size
    group_width = heads_here // kv_here
    query_rot = (
        apply_rotary(query, my_position, heads_here)
        .astype(jnp.bfloat16)
        .reshape(tok_rows, kv_here, group_width, head_size)
    )
    key_rotary = apply_rotary(key_projected, my_position, kv_here).astype(jnp.bfloat16)
    value_b = value_proj.astype(jnp.bfloat16)
    scale = head_size ** (-0.5)
    start_state = (
        jnp.full((kv_here, group_width, tok_rows), -1e30, jnp.float32),
        jnp.zeros((kv_here, group_width, tok_rows), jnp.float32),
        jnp.zeros((kv_here, group_width, tok_rows, head_size), jnp.float32),
    )
    state = start_state
    key_piece = lax.all_gather(key_rotary, "ctx", axis=0, tiled=True)
    value_piece = lax.all_gather(value_b, "ctx", axis=0, tiled=True)
    piece_rows = key_piece.shape[0]
    block_rows = math.gcd(piece_rows, 1024)
    block_count = piece_rows // block_rows
    key_blocks = key_piece.reshape(block_count, block_rows, kv_here, head_size)
    value_blocks = value_piece.reshape(block_count, block_rows, kv_here, head_size)
    key_positions = position_all.reshape(block_count, block_rows)
    key_segments = segment_all.reshape(block_count, block_rows)

    def advance(inner, item):
        key_block, value_block, block_positions, block_segments = item
        allowed = (block_positions[None, :] <= my_position[:, None]) & (
            block_segments[None, :] == my_segment[:, None]
        )
        running_max, running_sum, running_acc = inner
        scores = (
            jnp.einsum("tkgd,nkd->kgtn", query_rot, key_block, preferred_element_type=jnp.float32)
            * scale
        )
        scores = jnp.where(allowed[None, None], scores, -1e30)
        new_max = jnp.maximum(running_max, jnp.max(scores, axis=-1))
        exps = jnp.where(allowed[None, None], jnp.exp(scores - new_max[..., None]), 0.0)
        factor = jnp.exp(running_max - new_max)
        new_sum = running_sum * factor + jnp.sum(exps, axis=-1)
        new_acc = running_acc * factor[..., None] + jnp.einsum(
            "kgtn,nkd->kgtd",
            exps.astype(jnp.bfloat16),
            value_block,
            preferred_element_type=jnp.float32,
        )
        inner = (new_max, new_sum, new_acc)
        return (inner, None)

    state, _ = lax.scan(advance, state, (key_blocks, value_blocks, key_positions, key_segments))
    final_max, final_sum, final_acc = state
    mixed = final_acc / final_sum[..., None]
    return (
        jnp.transpose(mixed, (2, 0, 1, 3))
        .reshape(tok_rows, heads_here * head_size)
        .astype(jnp.bfloat16)
    )


def solution(mesh):
    return jax.shard_map(
        local,
        mesh=mesh,
        in_specs=(
            P(("groups", "ctx"), None),
            P(),
            P("ctx", "mp"),
            P("ctx", "mp"),
            P("ctx", "mp"),
            P("groups"),
            P("groups"),
        ),
        out_specs=P(("groups", "ctx"), "mp"),
        check_vma=False,
    )
```

profile of v0, /device:TPU:0, one launch (start us, length us, event | category | flops | bytes accessed | tf_op | source)
XLA Modules:
  0.0 256.6 jit_solution(9475699111471552098)
XLA Ops:
  6.5 0.7 all-gather.4.cloned.1.call-update
  7.3 0.7 all-gather.8.cloned.1.call-update
  8.1 0.7 all-gather.6.cloned.1.call-update
  9.0 0.4 multiply_cosine_fusion
  9.8 8.4 %gather_fusion = s32[1536]{0:T(1024)S(1)} fusion(s32[1536]{0:T(1024)S(1)} %copy-done, s32[2048]{0:T(1024)S(1)} %pad_clamp_fusion), kind=kCustom, calls=%fused_computation | custom fusion | bytes 18432 | tf_op jit(solution)/shard_map/jit(_take)/gather | solution.py:32
  18.2 5.0 %fusion.14 = f32[384]{0:T(512)S(1)} fusion(bf16[384,8192]{1,0:T(8,128)(2,1)} %param.9), kind=kLoop, calls=%fused_computation.27 | loop fusion | flops 9436800 | bytes 6292992 | tf_op jit(solution)/shard_map/reduce_sum | solution.py:36
  23.3 22.8 %all-gather.4.cloned.1.call-done = bf16[8192,256]{1,0:T(8,128)(2,1)} async-done(((bf16[2048,256]{1,0:T(8,128)(2,1)}), bf16[8192,256]{1,0:T(8,128)(2,1)}) %all-gather.4.cloned.1.call-update) | async-done | bytes 4194320 | tf_op jit(solution)/shard_map/all_gather | solution.py:46
  46.1 6.6 %fusion.22 = f32[384,256]{0,1:T(8,128)S(1)} fusion(bf16[8192,256]{1,0:T(8,128)(2,1)} %all-gather.4.cloned.1.call-done, bf16[384,8192]{1,0:T(8,128)(2,1)} %param.9, f32[8192]{0:T(1024)S(1)} %convert_element_type.38, f32[384]{0:T(512)S(1)} %add_rsqrt_fusion), kind=kOutput, calls=%fused_computation.54 | convolution fusion | flops 1623195648 | bytes 10913280 | tf_op jit(solution)/shard_map/dot_general | solution.py:45
  53.0 11.9 %all_gather.16 = bf16[1536,256]{1,0:T(8,128)(2,1)S(1)} all-gather(bf16[384,256]{1,0:T(8,128)(2,1)S(1)} %copy.25), channel_id=1, replica_groups=mesh['groups'=2,'ctx'=4,'mp'=4] {'ctx'}, dimensions={0}, use_global_device_ids=true | all-gather | bytes 983040 | tf_op jit(solution)/shard_map/all_gather | solution.py:71
  65.1 19.7 %all-gather.8.cloned.1.call-done = bf16[8192,256]{1,0:T(8,128)(2,1)} async-done(((bf16[2048,256]{1,0:T(8,128)(2,1)}), bf16[8192,256]{1,0:T(8,128)(2,1)}) %all-gather.8.cloned.1.call-update) | async-done | bytes 4194320 | tf_op jit(solution)/shard_map/all_gather | solution.py:50
  84.8 5.9 %convolution_convert_fusion = bf16[384,256]{1,0:T(8,128)(2,1)S(1)} fusion(bf16[8192,256]{1,0:T(8,128)(2,1)} %all-gather.8.cloned.1.call-done, bf16[384,8192]{1,0:T(8,128)(2,1)} %param.9, f32[8192]{0:T(1024)S(1)} %convert_element_type.38, f32[384]{0:T(512)S(1)} %add_rsqrt_fusion), kind=kOutput, calls=%fused_computation.34 | convolution fusion | flops 1623293952 | bytes 10716672 | tf_op jit(solution)/shard_map/dot_general | solution.py:48
  90.7 8.8 %all_gather.19 = bf16[1536,256]{1,0:T(8,128)(2,1)S(1)} all-gather(bf16[384,256]{1,0:T(8,128)(2,1)S(1)} %convolution_convert_fusion), channel_id=1, replica_groups=mesh['groups'=2,'ctx'=4,'mp'=4] {'ctx'}, dimensions={0}, use_global_device_ids=true | all-gather | bytes 983040 | tf_op jit(solution)/shard_map/all_gather | solution.py:72
  99.7 92.7 %all-gather.6.cloned.1.call-done = bf16[8192,1024]{1,0:T(8,128)(2,1)} async-done(((bf16[2048,1024]{1,0:T(8,128)(2,1)}), bf16[8192,1024]{1,0:T(8,128)(2,1)}) %all-gather.6.cloned.1.call-update) | async-done | bytes 16777232 | tf_op jit(solution)/shard_map/all_gather | solution.py:42
  192.3 12.4 %convolution_bitcast_fusion = f32[48,8,8,128]{3,1,2,0:T(8,128)S(1)} fusion(bf16[8192,1024]{1,0:T(8,128)(2,1)} %all-gather.6.cloned.1.call-done, bf16[384,8192]{1,0:T(8,128)(2,1)} %param.9, f32[8192]{0:T(1024)S(1)} %convert_element_type.38, f32[384]{0:T(512)S(1)} %add_rsqrt_fusion), kind=kOutput, calls=%fused_computation.33 | convolution fusion | flops 6455033856 | bytes 24675840 | tf_op jit(solution)/shard_map/dot_general | solution.py:40
  205.1 0.7 subtract_convert_fusion
  205.7 0.4 pad_maximum_fusion
  206.3 39.8 %while.15 = (s32[]{:T(128)}, f32[2,4,384]{2,1,0:T(4,128)S(1)}, f32[2,4,384]{2,1,0:T(4,128)S(1)}, f32[2,4,384,128]{3,2,1,0:T(8,128)}, s32[3,512]{1,0:T(4,128)S(1)...) while((s32[]{:T(128)}, f32[2,4,384]{2,1,0:T(4,128)S(1)}, ...), condition=%wide.region_4.5_spmd.clone, body=%wide.region_1.0_spmd.clone.sunk | while | flops 827538432 | bytes 50543788 | solution.py:105
  206.6 0.4 constant_dynamic-slice_fusion.7
  206.9 3.8 %fusion.37 = (f32[2,4,384]{2,1,0:T(4,128)S(1)}, f32[2,512,384,4]{2,1,3,0:T(8,128)}) fusion(pred[384,512]{0,1:T(8,128)(4,1)S(1)} %compare_and_fusion.2, bf16[384,2,4,128]{3,0,2,1:T(8,128)(2,1)S(1)} %get-tuple-element.281, bf16[1,512,2,128]{3,2,1,0:T(2,128)(2,1)S(1)} %get-tuple-element.240), kind=kOutput, calls=%fused_computation.3.clone.1 | convolution fusion | flops 407368704 | bytes 7548928 | tf_op jit(solution)/shard_map/while/body/eval_jaxpr/tkgd,nkd->kgtn/dot_general | solution.py:88
  210.8 4.4 %fusion.38 = f32[2,4,384]{2,1,0:T(4,128)S(1)} fusion(f32[2,512,384,4]{2,1,3,0:T(8,128)} %get-tuple-element.242, f32[2,4,384]{2,1,0:T(4,128)S(1)} %select_maximum_fusion.2, pred[384,512]{0,1:T(8,128)(4,1)S(1)} %compare_and_fusion.2), kind=kLoop, calls=%fused_computation.5.clone.1 | loop fusion | flops 7861248 | bytes 6512640 | tf_op jit(solution)/shard_map/while/body/eval_jaxpr/reduce_sum | solution.py:95
  215.4 3.4 %fusion.40 = f32[2,4,384,128]{3,2,1,0:T(8,128)} fusion(f32[2,4,384,128]{3,2,1,0:T(8,128)} %get-tuple-element.262, f32[2,512,384,4]{2,1,3,0:T(8,128)S(1)} %copy-done.1, f32[2,4,384]{2,1,0:T(4,128)S(1)} %select_maximum_fusion.2, pred[384,512]{0,1:T(8,128)(4,1)S(1)} %compare_and_fusion.2, f32[2,4,384]{2,1,0:T(4,128)S(1)} %get-tuple-element.244, ...), kind=kOutput, calls=%fused_computation.9.clone.1 | convolution fusion | flops 411697152 | bytes 9920513 | tf_op jit(solution)/shard_map/while/body/eval_jaxpr/kgtn,nkd->kgtd/dot_general | solution.py:96
  219.1 0.4 constant_dynamic-slice_fusion.7
  219.4 3.9 %fusion.37 = (f32[2,4,384]{2,1,0:T(4,128)S(1)}, f32[2,512,384,4]{2,1,3,0:T(8,128)}) fusion(pred[384,512]{0,1:T(8,128)(4,1)S(1)} %compare_and_fusion.2, bf16[384,2,4,128]{3,0,2,1:T(8,128)(2,1)S(1)} %get-tuple-element.281, bf16[1,512,2,128]{3,2,1,0:T(2,128)(2,1)S(1)} %get-tuple-element.240), kind=kOutput, calls=%fused_computation.3.clone.1 | convolution fusion | flops 407368704 | bytes 7548928 | tf_op jit(solution)/shard_map/while/body/eval_jaxpr/tkgd,nkd->kgtn/dot_general | solution.py:88
  223.3 4.4 %fusion.38 = f32[2,4,384]{2,1,0:T(4,128)S(1)} fusion(f32[2,512,384,4]{2,1,3,0:T(8,128)} %get-tuple-element.242, f32[2,4,384]{2,1,0:T(4,128)S(1)} %select_maximum_fusion.2, pred[384,512]{0,1:T(8,128)(4,1)S(1)} %compare_and_fusion.2), kind=kLoop, calls=%fused_computation.5.clone.1 | loop fusion | flops 7861248 | bytes 6512640 | tf_op jit(solution)/shard_map/while/body/eval_jaxpr/reduce_sum | solution.py:95
  227.9 4.6 %fusion.40 = f32[2,4,384,128]{3,2,1,0:T(8,128)} fusion(f32[2,4,384,128]{3,2,1,0:T(8,128)} %get-tuple-element.262, f32[2,512,384,4]{2,1,3,0:T(8,128)S(1)} %copy-done.1, f32[2,4,384]{2,1,0:T(4,128)S(1)} %select_maximum_fusion.2, pred[384,512]{0,1:T(8,128)(4,1)S(1)} %compare_and_fusion.2, f32[2,4,384]{2,1,0:T(4,128)S(1)} %get-tuple-element.244, ...), kind=kOutput, calls=%fused_computation.9.clone.1 | convolution fusion | flops 411697152 | bytes 9920513 | tf_op jit(solution)/shard_map/while/body/eval_jaxpr/kgtn,nkd->kgtd/dot_general | solution.py:96
  232.7 0.4 constant_dynamic-slice_fusion.7
  233.1 3.8 %fusion.37 = (f32[2,4,384]{2,1,0:T(4,128)S(1)}, f32[2,512,384,4]{2,1,3,0:T(8,128)}) fusion(pred[384,512]{0,1:T(8,128)(4,1)S(1)} %compare_and_fusion.2, bf16[384,2,4,128]{3,0,2,1:T(8,128)(2,1)S(1)} %get-tuple-element.281, bf16[1,512,2,128]{3,2,1,0:T(2,128)(2,1)S(1)} %get-tuple-element.240), kind=kOutput, calls=%fused_computation.3.clone.1 | convolution fusion | flops 407368704 | bytes 7548928 | tf_op jit(solution)/shard_map/while/body/eval_jaxpr/tkgd,nkd->kgtn/dot_general | solution.py:88
  236.9 4.4 %fusion.38 = f32[2,4,384]{2,1,0:T(4,128)S(1)} fusion(f32[2,512,384,4]{2,1,3,0:T(8,128)} %get-tuple-element.242, f32[2,4,384]{2,1,0:T(4,128)S(1)} %select_maximum_fusion.2, pred[384,512]{0,1:T(8,128)(4,1)S(1)} %compare_and_fusion.2), kind=kLoop, calls=%fused_computation.5.clone.1 | loop fusion | flops 7861248 | bytes 6512640 | tf_op jit(solution)/shard_map/while/body/eval_jaxpr/reduce_sum | solution.py:95
  241.5 4.6 %fusion.40 = f32[2,4,384,128]{3,2,1,0:T(8,128)} fusion(f32[2,4,384,128]{3,2,1,0:T(8,128)} %get-tuple-element.262, f32[2,512,384,4]{2,1,3,0:T(8,128)S(1)} %copy-done.1, f32[2,4,384]{2,1,0:T(4,128)S(1)} %select_maximum_fusion.2, pred[384,512]{0,1:T(8,128)(4,1)S(1)} %compare_and_fusion.2, f32[2,4,384]{2,1,0:T(4,128)S(1)} %get-tuple-element.244, ...), kind=kOutput, calls=%fused_computation.9.clone.1 | convolution fusion | flops 411697152 | bytes 9920513 | tf_op jit(solution)/shard_map/while/body/eval_jaxpr/kgtn,nkd->kgtd/dot_general | solution.py:96
  246.1 1.9 fusion.17
  248.0 0.6 copy.21
  248.6 1.4 convert_element_type.46
  (56 shorter events, 2.9 us)
Async XLA Ops:
  6.5 3.2 %copy-start = (s32[1536]{0:T(1024)S(1)}, s32[1536]{0:T(1024)}, u32[]{:S(2)}) copy-start(s32[1536]{0:T(1024)} %param.15) | copy-start | bytes 18436
  6.5 2.2 copy-start.3
  6.5 3.1 %copy-start.2 = (bf16[8192]{0:T(1024)(128)(2,1)S(1)}, bf16[8192]{0:T(1024)(128)(2,1)}, u32[]{:S(2)}) copy-start(bf16[8192]{0:T(1024)(128)(2,1)} %param.10) | copy-start | bytes 49156
  6.5 39.6 %all-gather.4.cloned.1.call-start = ((), (), s32[]{:S(2)}) async-start(), calls=%async_computation | async-start | bytes 5242880 | tf_op jit(solution)/shard_map/all_gather | solution.py:46
  7.3 77.5 %all-gather.8.cloned.1.call-start = ((), (), s32[]{:S(2)}) async-start(), calls=%async_computation.2 | async-start | bytes 5242880 | tf_op jit(solution)/shard_map/all_gather | solution.py:50
  8.0 184.3 %all-gather.6.cloned.1.call-start = ((), (), s32[]{:S(2)}) async-start(), calls=%async_computation.1 | async-start | bytes 20971520 | tf_op jit(solution)/shard_map/all_gather | solution.py:42
  210.8 4.6 %copy-start.1 = (f32[2,512,384,4]{2,1,3,0:T(8,128)S(1)}, f32[2,512,384,4]{2,1,3,0:T(8,128)}, u32[]{:S(2)}) copy-start(f32[2,512,384,4]{2,1,3,0:T(8,128)} %get-tuple-element.242) | copy-start | bytes 18874372 | tf_op jit(solution)/shard_map/while
  223.3 4.6 %copy-start.1 = (f32[2,512,384,4]{2,1,3,0:T(8,128)S(1)}, f32[2,512,384,4]{2,1,3,0:T(8,128)}, u32[]{:S(2)}) copy-start(f32[2,512,384,4]{2,1,3,0:T(8,128)} %get-tuple-element.242) | copy-start | bytes 18874372 | tf_op jit(solution)/shard_map/while
  236.9 4.6 %copy-start.1 = (f32[2,512,384,4]{2,1,3,0:T(8,128)S(1)}, f32[2,512,384,4]{2,1,3,0:T(8,128)}, u32[]{:S(2)}) copy-start(f32[2,512,384,4]{2,1,3,0:T(8,128)} %get-tuple-element.242) | copy-start | bytes 18874372 | tf_op jit(solution)/shard_map/while
Sparse Core Ops, SparseCore 0:
  8.9 37.1 all-gather.3
  47.7 37.0 all-gather.7
  86.4 105.9 all-gather.5
where the time goes:
time: 257 us
  waiting for transfers between devices  137 us (53%)
  matrix products  48.9 us (19%)
  other arithmetic  22.9 us (9%)
  blocking collectives  20.7 us (8%)
  between operations  13.3 us (5%)
  local copies, waits for them, and re-layouts  13.2 us (5%)
    all_gather x1, waiting for transfers between devices, local(): lax.all_gather(w_query, 'ctx', axis=0, tiled=True)  92.7 us
    all_gather x1, waiting for transfers between devices, local(): lax.all_gather(w_key, 'ctx', axis=0, tiled=True)  22.8 us
    all_gather x1, waiting for transfers between devices, local(): lax.all_gather(value_weight, 'ctx', axis=0, tiled=True)  19.7 us
    reduce_sum x3, other arithmetic, advance(): new_sum = running_sum * factor + jnp.sum(exps, axis=-1)  13.3 us
    dot_general x3, matrix products, advance(): jnp.einsum('kgtn,nkd->kgtd', exps.astype(jnp.bfloat16), value_block, pref...  12.5 us
    dot_general x1, matrix products, local(): jnp.dot(normed, lax.all_gather(w_query, 'ctx', axis=0, tiled=True), prefe...  12.4 us
    all_gather x1, blocking collectives, local(): key_piece = lax.all_gather(key_rotary, 'ctx', axis=0, tiled=True)  11.9 us
    dot_general x3, matrix products, advance(): jnp.einsum('tkgd,nkd->kgtn', query_rot, key_block, preferred_element_type...  11.5 us
  transfers between devices with their start and end apart: 3, of which 3 were waited for; matrix products, arithmetic and copies ran while one was open for 11% of the time, Pallas kernels for 0%

commit v1 on v0

--- a/solution.py
+++ b/solution.py
@@ -68,8 +68,11 @@
         jnp.zeros((kv_here, group_width, tok_rows, head_size), jnp.float32),
     )
     state = start_state
-    key_piece = lax.all_gather(key_rotary, "ctx", axis=0, tiled=True)
-    value_piece = lax.all_gather(value_b, "ctx", axis=0, tiled=True)
+    key_piece, value_piece = jnp.split(
+        lax.all_gather(jnp.concatenate([key_rotary, value_b], axis=1), "ctx", axis=0, tiled=True),
+        [key_rotary.shape[1]],
+        axis=1,
+    )
     piece_rows = key_piece.shape[0]
     block_rows = math.gcd(piece_rows, 1024)
     block_count = piece_rows // block_rows

time: 257 us -> 277 us (1.078)
  waiting for transfers between devices: 137 us -> 176 us
  blocking collectives: 20.7 us -> 0 us
  local copies, waits for them, and re-layouts: 13.2 us -> 16.7 us
    all_gather x2 -> x0, blocking collectives: 20.7 us -> none  [the longest x1 11.9 us: local(): key_piece = lax.all_gather(key_rotary, 'ctx', axis=0, tiled=True)]
    all_gather x0 -> x1, waiting for transfers between devices: none -> 10.2 us  [local(): lax.all_gather(jnp.concatenate([key_rotary, value_b], axis=1), 'ctx', axi...]
    all_gather x1, waiting for transfers between devices: 92.7 us -> 102 us  [local(): lax.all_gather(w_query, 'ctx', axis=0, tiled=True)]
    all_gather x1, waiting for transfers between devices: 19.7 us -> 29.4 us  [local(): lax.all_gather(value_weight, 'ctx', axis=0, tiled=True)]
    all_gather x1, waiting for transfers between devices: 22.8 us -> 32 us  [local(): lax.all_gather(w_key, 'ctx', axis=0, tiled=True)]
  transfers between devices with their start and end apart: 3 -> 4, of which waited for: 3 -> 4; matrix products, arithmetic and copies ran while one was open for 11% -> 10% of each run, Pallas kernels for 0% -> 0%
where the time goes in v1:
time: 277 us
  waiting for transfers between devices  176 us (64%)
  matrix products  47.6 us (17%)
  other arithmetic  22.8 us (8%)
  local copies, waits for them, and re-layouts  16.7 us (6%)
  between operations  13.3 us (5%)
    all_gather x1, waiting for transfers between devices, local(): lax.all_gather(w_query, 'ctx', axis=0, tiled=True)  102 us
    all_gather x1, waiting for transfers between devices, local(): lax.all_gather(w_key, 'ctx', axis=0, tiled=True)  32 us
    all_gather x1, waiting for transfers between devices, local(): lax.all_gather(value_weight, 'ctx', axis=0, tiled=True)  29.4 us
    reduce_sum x3, other arithmetic, advance(): new_sum = running_sum * factor + jnp.sum(exps, axis=-1)  13.4 us
    dot_general x1, matrix products, local(): jnp.dot(normed, lax.all_gather(w_query, 'ctx', axis=0, tiled=True), prefe...  12.2 us
    dot_general x3, matrix products, advance(): jnp.einsum('tkgd,nkd->kgtn', query_rot, key_block, preferred_element_type...  11.4 us
    dot_general x3, matrix products, advance(): jnp.einsum('kgtn,nkd->kgtd', exps.astype(jnp.bfloat16), value_block, pref...  10.8 us
    all_gather x1, waiting for transfers between devices, local(): lax.all_gather(jnp.concatenate([key_rotary, value_b], axis=1), 'ctx', axi...  10.2 us
  transfers between devices with their start and end apart: 4, of which 4 were waited for; matrix products, arithmetic and copies ran while one was open for 10% of the time, Pallas kernels for 0%

profile of v1, /device:TPU:0, one launch (start us, length us, event | category | flops | bytes accessed | tf_op | source)
XLA Modules:
  0.0 276.6 jit_solution(157070263941900255)
XLA Ops:
  6.5 0.7 all-gather.5.cloned.1.call-update
  7.3 0.7 all-gather.7.cloned.1.call-update
  8.1 0.7 broadcast_multiply_fusion
  8.8 0.7 convert_element_type.38
  9.6 4.1 %fusion.20 = f32[384]{0:T(512)S(1)} fusion(bf16[384,8192]{1,0:T(8,128)(2,1)} %param.9), kind=kLoop, calls=%fused_computation.29 | loop fusion | flops 9436800 | bytes 6292992 | tf_op jit(solution)/shard_map/reduce_sum | solution.py:36
  14.2 32.0 %all-gather.5.cloned.1.call-done = bf16[8192,256]{1,0:T(8,128)(2,1)} async-done(((bf16[2048,256]{1,0:T(8,128)(2,1)}), bf16[8192,256]{1,0:T(8,128)(2,1)}) %all-gather.5.cloned.1.call-update) | async-done | bytes 4194320 | tf_op jit(solution)/shard_map/all_gather | solution.py:46
  46.1 6.6 %fusion.28 = f32[384,256]{0,1:T(8,128)S(1)} fusion(bf16[8192,256]{1,0:T(8,128)(2,1)} %all-gather.5.cloned.1.call-done, bf16[384,8192]{1,0:T(8,128)(2,1)} %param.9, f32[8192]{0:T(1024)S(1)} %convert_element_type.38, f32[384]{0:T(512)S(1)} %add_rsqrt_fusion), kind=kOutput, calls=%fused_computation.57 | convolution fusion | flops 1623195648 | bytes 10913280 | tf_op jit(solution)/shard_map/dot_general | solution.py:45
  52.8 29.4 %all-gather.7.cloned.1.call-done = bf16[8192,256]{1,0:T(8,128)(2,1)} async-done(((bf16[2048,256]{1,0:T(8,128)(2,1)}), bf16[8192,256]{1,0:T(8,128)(2,1)}) %all-gather.7.cloned.1.call-update) | async-done | bytes 4194320 | tf_op jit(solution)/shard_map/all_gather | solution.py:50
  82.2 6.6 %convolution_convert_fusion = bf16[384,256]{0,1:T(8,128)(2,1)S(1)} fusion(bf16[8192,256]{1,0:T(8,128)(2,1)} %all-gather.7.cloned.1.call-done, bf16[384,8192]{1,0:T(8,128)(2,1)} %param.9, f32[8192]{0:T(1024)S(1)} %convert_element_type.38, f32[384]{0:T(512)S(1)} %add_rsqrt_fusion), kind=kOutput, calls=%fused_computation.36 | convolution fusion | flops 1623293952 | bytes 10716672 | tf_op jit(solution)/shard_map/dot_general | solution.py:48
  88.8 0.8 pad_maximum_fusion.1
  90.6 8.6 %gather_fusion = s32[1536]{0:T(1024)S(1)} fusion(s32[1536]{0:T(1024)S(1)} %copy-done, s32[2048]{0:T(1024)S(1)} %pad_clamp_fusion), kind=kCustom, calls=%fused_computation | custom fusion | bytes 18432 | tf_op jit(solution)/shard_map/jit(_take)/gather | solution.py:32
  99.3 10.2 %all-gather.9.cloned.1.call-done = bf16[1536,512]{0,1:T(8,128)(2,1)} async-done(((bf16[384,512]{0,1:T(8,128)(2,1)}), bf16[1536,512]{0,1:T(8,128)(2,1)}) %all-gather.9.cloned.1.call-update) | async-done | bytes 1572880 | tf_op jit(solution)/shard_map/all_gather | solution.py:72
  109.5 1.5 fusion.31
  110.9 0.6 reshape.201
  111.5 0.8 copy.21
  112.3 0.6 reshape.202
  112.9 1.5 copy.22
  114.4 102.4 %all-gather.11.cloned.1.call-done = bf16[8192,1024]{1,0:T(8,128)(2,1)} async-done(((bf16[2048,1024]{1,0:T(8,128)(2,1)}), bf16[8192,1024]{1,0:T(8,128)(2,1)}) %all-gather.11.cloned.1.call-update) | async-done | bytes 16777232 | tf_op jit(solution)/shard_map/all_gather | solution.py:42
  216.8 12.2 %convolution_bitcast_fusion = f32[48,8,8,128]{3,1,2,0:T(8,128)S(1)} fusion(bf16[8192,1024]{1,0:T(8,128)(2,1)} %all-gather.11.cloned.1.call-done, bf16[384,8192]{1,0:T(8,128)(2,1)} %param.9, f32[8192]{0:T(1024)S(1)} %convert_element_type.38, f32[384]{0:T(512)S(1)} %add_rsqrt_fusion), kind=kOutput, calls=%fused_computation.35 | convolution fusion | flops 6455033856 | bytes 24675840 | tf_op jit(solution)/shard_map/dot_general | solution.py:40
  229.4 0.7 subtract_convert_fusion
  230.7 36.8 %while.15 = (s32[]{:T(128)}, f32[2,4,384]{2,1,0:T(4,128)S(1)}, f32[2,4,384]{2,1,0:T(4,128)S(1)}, f32[2,4,384,128]{3,2,1,0:T(8,128)S(1)}, s32[3,512]{1,0:T(4,128)...) while((s32[]{:T(128)}, f32[2,4,384]{2,1,0:T(4,128)S(1)}, ...), condition=%wide.region_4.5_spmd.clone, body=%wide.region_1.0_spmd.clone.sunk | while | flops 827538432 | bytes 49495724 | solution.py:108
  231.0 3.8 %fusion.46 = (f32[2,4,384]{2,1,0:T(4,128)S(1)}, f32[2,512,384,4]{2,1,3,0:T(8,128)}) fusion(pred[384,512]{0,1:T(8,128)(4,1)S(1)} %compare_and_fusion.2, bf16[384,2,4,128]{3,0,2,1:T(8,128)(2,1)S(1)} %get-tuple-element.277, bf16[3,512,2,128]{3,1,2,0:T(8,128)(2,1)S(1)} %get-tuple-element.276, s32[]{:T(128)} %get-tuple-element.255), kind=kOutput, calls=%fused_computation.3.clone.1 | convolution fusion | flops 407368704 | bytes 7548932 | tf_op jit(solution)/shard_map/while/body/eval_jaxpr/tkgd,nkd->kgtn/dot_general | solution.py:91
  234.8 4.5 %fusion.47 = f32[2,4,384]{2,1,0:T(4,128)S(1)} fusion(f32[2,512,384,4]{2,1,3,0:T(8,128)} %get-tuple-element.239, f32[2,4,384]{2,1,0:T(4,128)S(1)} %select_maximum_fusion.2, pred[384,512]{0,1:T(8,128)(4,1)S(1)} %compare_and_fusion.2), kind=kLoop, calls=%fused_computation.5.clone.1 | loop fusion | flops 7861248 | bytes 6512640 | tf_op jit(solution)/shard_map/while/body/eval_jaxpr/reduce_sum | solution.py:98
  239.3 3.6 %fusion.49 = f32[2,4,384,128]{3,2,1,0:T(8,128)S(1)} fusion(f32[2,4,384,128]{3,2,1,0:T(8,128)S(1)} %get-tuple-element.258, f32[2,512,384,4]{2,1,3,0:T(8,128)S(1)} %copy-done.1, f32[2,4,384]{2,1,0:T(4,128)S(1)} %select_maximum_fusion.2, pred[384,512]{0,1:T(8,128)(4,1)S(1)} %compare_and_fusion.2, f32[2,4,384]{2,1,0:T(4,128)S(1)} %get-tuple-element.241, ...), kind=kOutput, calls=%fused_computation.9.clone.1 | convolution fusion | flops 411697152 | bytes 9921025 | tf_op jit(solution)/shard_map/while/body/eval_jaxpr/kgtn,nkd->kgtd/dot_general | solution.py:99
  243.2 3.8 %fusion.46 = (f32[2,4,384]{2,1,0:T(4,128)S(1)}, f32[2,512,384,4]{2,1,3,0:T(8,128)}) fusion(pred[384,512]{0,1:T(8,128)(4,1)S(1)} %compare_and_fusion.2, bf16[384,2,4,128]{3,0,2,1:T(8,128)(2,1)S(1)} %get-tuple-element.277, bf16[3,512,2,128]{3,1,2,0:T(8,128)(2,1)S(1)} %get-tuple-element.276, s32[]{:T(128)} %get-tuple-element.255), kind=kOutput, calls=%fused_computation.3.clone.1 | convolution fusion | flops 407368704 | bytes 7548932 | tf_op jit(solution)/shard_map/while/body/eval_jaxpr/tkgd,nkd->kgtn/dot_general | solution.py:91
  247.0 4.5 %fusion.47 = f32[2,4,384]{2,1,0:T(4,128)S(1)} fusion(f32[2,512,384,4]{2,1,3,0:T(8,128)} %get-tuple-element.239, f32[2,4,384]{2,1,0:T(4,128)S(1)} %select_maximum_fusion.2, pred[384,512]{0,1:T(8,128)(4,1)S(1)} %compare_and_fusion.2), kind=kLoop, calls=%fused_computation.5.clone.1 | loop fusion | flops 7861248 | bytes 6512640 | tf_op jit(solution)/shard_map/while/body/eval_jaxpr/reduce_sum | solution.py:98
  251.6 3.6 %fusion.49 = f32[2,4,384,128]{3,2,1,0:T(8,128)S(1)} fusion(f32[2,4,384,128]{3,2,1,0:T(8,128)S(1)} %get-tuple-element.258, f32[2,512,384,4]{2,1,3,0:T(8,128)S(1)} %copy-done.1, f32[2,4,384]{2,1,0:T(4,128)S(1)} %select_maximum_fusion.2, pred[384,512]{0,1:T(8,128)(4,1)S(1)} %compare_and_fusion.2, f32[2,4,384]{2,1,0:T(4,128)S(1)} %get-tuple-element.241, ...), kind=kOutput, calls=%fused_computation.9.clone.1 | convolution fusion | flops 411697152 | bytes 9921025 | tf_op jit(solution)/shard_map/while/body/eval_jaxpr/kgtn,nkd->kgtd/dot_general | solution.py:99
  255.5 3.8 %fusion.46 = (f32[2,4,384]{2,1,0:T(4,128)S(1)}, f32[2,512,384,4]{2,1,3,0:T(8,128)}) fusion(pred[384,512]{0,1:T(8,128)(4,1)S(1)} %compare_and_fusion.2, bf16[384,2,4,128]{3,0,2,1:T(8,128)(2,1)S(1)} %get-tuple-element.277, bf16[3,512,2,128]{3,1,2,0:T(8,128)(2,1)S(1)} %get-tuple-element.276, s32[]{:T(128)} %get-tuple-element.255), kind=kOutput, calls=%fused_computation.3.clone.1 | convolution fusion | flops 407368704 | bytes 7548932 | tf_op jit(solution)/shard_map/while/body/eval_jaxpr/tkgd,nkd->kgtn/dot_general | solution.py:91
  259.3 4.5 %fusion.47 = f32[2,4,384]{2,1,0:T(4,128)S(1)} fusion(f32[2,512,384,4]{2,1,3,0:T(8,128)} %get-tuple-element.239, f32[2,4,384]{2,1,0:T(4,128)S(1)} %select_maximum_fusion.2, pred[384,512]{0,1:T(8,128)(4,1)S(1)} %compare_and_fusion.2), kind=kLoop, calls=%fused_computation.5.clone.1 | loop fusion | flops 7861248 | bytes 6512640 | tf_op jit(solution)/shard_map/while/body/eval_jaxpr/reduce_sum | solution.py:98
  263.9 3.6 %fusion.49 = f32[2,4,384,128]{3,2,1,0:T(8,128)S(1)} fusion(f32[2,4,384,128]{3,2,1,0:T(8,128)S(1)} %get-tuple-element.258, f32[2,512,384,4]{2,1,3,0:T(8,128)S(1)} %copy-done.1, f32[2,4,384]{2,1,0:T(4,128)S(1)} %select_maximum_fusion.2, pred[384,512]{0,1:T(8,128)(4,1)S(1)} %compare_and_fusion.2, f32[2,4,384]{2,1,0:T(4,128)S(1)} %get-tuple-element.241, ...), kind=kOutput, calls=%fused_computation.9.clone.1 | convolution fusion | flops 411697152 | bytes 9921025 | tf_op jit(solution)/shard_map/while/body/eval_jaxpr/kgtn,nkd->kgtd/dot_general | solution.py:99
  268.0 0.6 copy.23
  268.6 1.4 convert_element_type.46
  (55 shorter events, 4.2 us)
Async XLA Ops:
  6.5 84.0 %copy-start = (s32[1536]{0:T(1024)S(1)}, s32[1536]{0:T(1024)}, u32[]{:S(2)}) copy-start(s32[1536]{0:T(1024)} %param.15) | copy-start | bytes 18436
  6.5 39.6 %all-gather.5.cloned.1.call-start = ((), (), s32[]{:S(2)}) async-start(), calls=%async_computation | async-start | bytes 5242880 | tf_op jit(solution)/shard_map/all_gather | solution.py:46
  7.3 74.9 %all-gather.7.cloned.1.call-start = ((), (), s32[]{:S(2)}) async-start(), calls=%async_computation.1 | async-start | bytes 5242880 | tf_op jit(solution)/shard_map/all_gather | solution.py:50
  8.0 101.4 %all-gather.9.cloned.1.call-start = ((), (), s32[]{:S(2)}) async-start(), calls=%async_computation.2 | async-start | bytes 1966080 | tf_op jit(solution)/shard_map/all_gather | solution.py:72
  89.6 127.2 %all-gather.11.cloned.1.call-start = ((), (), s32[]{:S(2)}) async-start(), calls=%async_computation.3 | async-start | bytes 20971520 | tf_op jit(solution)/shard_map/all_gather | solution.py:42
  229.1 1.6 copy-start.2
  234.7 4.6 %copy-start.1 = (f32[2,512,384,4]{2,1,3,0:T(8,128)S(1)}, f32[2,512,384,4]{2,1,3,0:T(8,128)}, u32[]{:S(2)}) copy-start(f32[2,512,384,4]{2,1,3,0:T(8,128)} %get-tuple-element.239) | copy-start | bytes 18874372 | tf_op jit(solution)/shard_map/while
  247.0 4.6 %copy-start.1 = (f32[2,512,384,4]{2,1,3,0:T(8,128)S(1)}, f32[2,512,384,4]{2,1,3,0:T(8,128)}, u32[]{:S(2)}) copy-start(f32[2,512,384,4]{2,1,3,0:T(8,128)} %get-tuple-element.239) | copy-start | bytes 18874372 | tf_op jit(solution)/shard_map/while
  259.3 4.6 %copy-start.1 = (f32[2,512,384,4]{2,1,3,0:T(8,128)S(1)}, f32[2,512,384,4]{2,1,3,0:T(8,128)}, u32[]{:S(2)}) copy-start(f32[2,512,384,4]{2,1,3,0:T(8,128)} %get-tuple-element.239) | copy-start | bytes 18874372 | tf_op jit(solution)/shard_map/while
Sparse Core Ops, SparseCore 0:
  8.9 37.1 all-gather.4
  47.7 34.4 all-gather.6
  89.7 19.6 all-gather.8
  110.9 105.9 all-gather.10
